TPU v7x, 128 devices: a whole 4x4x4 slice. The times are simulated.
128 devices in a mesh: bx: 32 (over x, z, core), by: 2 (over y_hi), col: 2 (over y_lo).
Axes of the slice: x: 4, y: 4 (y_hi: 2, y_lo: 2; y = y_hi * 2 + y_lo), z: 4, core: 2. Of those that a mesh axis runs over, the one named last changes fastest.
Arguments:
- multipoles: bfloat16 [2, 152, 32, 1024], P(None, 'col', 'bx', 'by'), may hold values from -6 to 6
- kernel: bfloat16 [2, 32, 32, 17, 152, 152], P(None, 'bx', 'by', None, 'col'), may hold values from -0.5 to 0.5
Outputs:
- locals_out: float32 [2, 152, 32, 1024], P(None, 'col', 'bx', 'by')
All inputs are finite; a program needn't handle non-finite values.
Results may differ from a plain program's by a relative error of at most 0.0029.
Values may be sent and summed in bfloat16 or wider, within the bound.
No kernel may reach another device: no remote copies, remote signals or barrier semaphores. Data moves between devices by JAX's collectives and lax.ppermute only.
A program may use at most 128 MiB of HBM per device.

v0:
```python
import math
import jax
import jax.numpy as jnp
from jax import lax
from jax.sharding import PartitionSpec as P

NB = 32
KZ = 17
precise = lax.Precision.HIGHEST


def angle_table(count_in, count_out):
    left_index = jnp.arange(count_in, dtype=jnp.int32)[:, None]
    second = jnp.arange(count_out, dtype=jnp.int32)[None, :]
    phases = (left_index * second % count_in).astype(jnp.float32) * (2.0 * math.pi / count_in)
    return (jnp.cos(phases), jnp.sin(phases))


def contract(pattern, values, table):
    return jnp.einsum(pattern, values, table, precision=precise)


def to_planes(spatial):
    return lax.all_to_all(
        lax.all_to_all(spatial, "bx", split_axis=4, concat_axis=2, tiled=True),
        "by",
        split_axis=0,
        concat_axis=3,
        tiled=True,
    )


def to_columns(waves):
    return lax.all_to_all(
        lax.all_to_all(waves, "bx", split_axis=3, concat_axis=5, tiled=True),
        "by",
        split_axis=4,
        concat_axis=1,
        tiled=True,
    )


def back_planes(columns):
    return lax.all_to_all(
        lax.all_to_all(columns, "bx", split_axis=5, concat_axis=3, tiled=True),
        "by",
        split_axis=1,
        concat_axis=4,
        tiled=True,
    )


def back_boxes(planes):
    return lax.all_to_all(
        lax.all_to_all(planes, "bx", split_axis=2, concat_axis=4, tiled=True),
        "by",
        split_axis=3,
        concat_axis=0,
        tiled=True,
    )


def kernel_terms(kernel_part, panel):
    pattern = "abkij,rjabk->riabk"
    real_part = jnp.einsum(
        pattern, kernel_part[0], panel[0], preferred_element_type=jnp.float32
    ) - jnp.einsum(pattern, kernel_part[1], panel[1], preferred_element_type=jnp.float32)
    imag_part = jnp.einsum(
        pattern, kernel_part[0], panel[1], preferred_element_type=jnp.float32
    ) + jnp.einsum(pattern, kernel_part[1], panel[0], preferred_element_type=jnp.float32)
    return (real_part, imag_part)


def apply_kernel(spectrum, kernel):
    panels = lax.all_gather(spectrum, "col", axis=2, tiled=True)
    return kernel_terms(kernel, panels)


def on_device(multipoles, kernel):
    rhs_count, coeffs, x_local, plane_cells = multipoles.shape
    grid_side = NB
    cos_grid, sin_grid = angle_table(grid_side, grid_side)
    cos_half, sin_half = angle_table(grid_side, KZ)
    spatial_raw = multipoles.reshape(
        rhs_count, coeffs, x_local, plane_cells // grid_side, grid_side
    )
    along_x = "rcxyz,xk->rckyz"
    along_y = "rckyz,yl->rcklz"
    planes = to_planes(spatial_raw).astype(jnp.float32)
    first_re = contract(along_x, planes, cos_grid)
    first_im = -contract(along_x, planes, sin_grid)
    wave_re = contract(along_y, first_re, cos_grid) + contract(along_y, first_im, sin_grid)
    wave_im = contract(along_y, first_im, cos_grid) - contract(along_y, first_re, sin_grid)
    columns = to_columns(jnp.stack([wave_re, wave_im]))
    along_z = "rcabz,zk->rcabk"
    spec_re = contract(along_z, columns[0], cos_half) + contract(along_z, columns[1], sin_half)
    spec_im = contract(along_z, columns[1], cos_half) - contract(along_z, columns[0], sin_half)
    spectrum = jnp.stack([spec_re, spec_im]).astype(jnp.bfloat16)
    local_re, local_im = apply_kernel(spectrum, kernel)
    freq_index = jnp.arange(KZ, dtype=jnp.int32)
    weights = jnp.where((freq_index == 0) | (freq_index == grid_side // 2), 1.0, 2.0).astype(
        jnp.float32
    )
    cos_back = cos_half * weights[None, :]
    sin_back = sin_half * weights[None, :]
    from_z = "rcabk,zk->rcabz"
    back_re = contract(from_z, local_re, cos_back) - contract(from_z, local_im, sin_back)
    back_im = contract(from_z, local_re, sin_back) + contract(from_z, local_im, cos_back)
    planes_back = back_planes(jnp.stack([back_re, back_im]))
    turn_re = contract(along_x, planes_back[0], cos_grid) - contract(
        along_x, planes_back[1], sin_grid
    )
    turn_im = contract(along_x, planes_back[0], sin_grid) + contract(
        along_x, planes_back[1], cos_grid
    )
    spatial_out = (contract(along_y, turn_re, cos_grid) - contract(along_y, turn_im, sin_grid)) * (
        1.0 / float(grid_side**3)
    )
    result = back_boxes(spatial_out)
    return result.reshape(rhs_count, coeffs, x_local, plane_cells)


def solution(mesh):
    placed = (P(None, "col", "bx", "by"), P(None, "bx", "by", None, "col", None))
    return jax.shard_map(
        on_device, mesh=mesh, in_specs=placed, out_specs=P(None, "col", "bx", "by"), check_vma=False
    )
```

profile of v0, /device:TPU:1, one launch (start us, length us, event | category | flops | bytes accessed | tf_op | source)
XLA Modules:
  0.0 250.1 jit_solution(13036597349925570126)
XLA Ops:
  0.0 1.1 copy.42
  1.2 18.2 %all_to_all.132 = bf16[2,76,1,16,32]{1,3,0,2,4:T(8,128)(2,1)S(1)} all-to-all(bf16[2,76,1,16,32]{1,3,0,2,4:T(8,128)(2,1)S(1)} %copy.43), channel_id=1, replica_groups=mesh['bx'=32,'by'=2,'col'=2] {'bx'}, dimensions={4} | all-to-all | bytes 311296 | tf_op jit(solution)/shard_map/all_to_all | solution.py:25
  19.5 10.3 %all_to_all.133 = bf16[2,76,32,16,1]{1,2,3,4,0:T(8,128)(2,1)S(1)} all-to-all(bf16[2,76,32,16,1]{1,2,3,4,0:T(8,128)(2,1)S(1)} %copy.44), channel_id=1, replica_groups=mesh['bx'=32,'by'=2,'col'=2] {'by'}, dimensions={0} | all-to-all | bytes 311296 | tf_op jit(solution)/shard_map/all_to_all | solution.py:24
  31.6 0.9 fusion.38
  32.5 0.9 fusion.16
  34.5 21.3 %all_to_all.134 = f32[2,1,76,32,32,1]{2,4,5,1,0,3:T(8,128)S(1)} all-to-all(f32[2,1,76,32,32,1]{2,4,5,1,0,3:T(8,128)S(1)} %copy.49), channel_id=1, replica_groups=mesh['bx'=32,'by'=2,'col'=2] {'bx'}, dimensions={3} | all-to-all | bytes 1245184 | tf_op jit(solution)/shard_map/all_to_all | solution.py:35
  55.8 1.6 copy.50
  57.4 3.6 %all-to-all-start.3 = ((f32[2,1,76,1,32,32]{2,5,0,3,1,4:T(8,128)}), f32[2,1,76,1,32,32]{2,5,0,3,1,4:T(8,128)S(1)}, u32[]{:S(2)}, u32[]{:S(2)}) async-start(f32[2,1,76,1,32,32]{2,5,0,3,1,4:T(8,128)} %copy.50), calls=%async_computation.3 | async-start | bytes 2097152 | tf_op jit(solution)/shard_map/all_to_all | solution.py:34
  61.0 15.2 %fusion.200 = (bf16[1,1,16,17,76,152]{5,2,4,3,1,0:T(8,128)(2,1)}, bf16[1,1,16,17,76,152]{5,2,4,3,1,0:T(8,128)(2,1)}) fusion(bf16[2,1,16,17,76,152]{5,2,4,3,1,0:T(8,128)(2,1)} %param.3), kind=kLoop, calls=%fused_computation.195 | loop fusion | bytes 25137152 | tf_op jit(solution)/shard_map/slice | solution.py:66
  76.2 18.9 %copy.73 = bf16[1,1,16,17,76,152]{4,5,3,2,1,0:T(8,128)(2,1)} copy(bf16[1,1,16,17,76,152]{5,2,4,3,1,0:T(8,128)(2,1)} %get-tuple-element.5) | data formatting | bytes 12568576
  95.1 18.8 %copy.75 = bf16[1,1,16,17,76,152]{4,5,3,2,1,0:T(8,128)(2,1)} copy(bf16[1,1,16,17,76,152]{5,2,4,3,1,0:T(8,128)(2,1)} %get-tuple-element.6) | data formatting | bytes 12568576
  116.4 2.2 copy.52
  118.6 29.5 %all_gather.3 = bf16[2,2,152,1,16,17]{5,4,3,1,0,2:T(8,128)(2,1)S(1)} all-gather(bf16[2,2,76,1,16,17]{5,4,3,1,0,2:T(8,128)(2,1)S(1)} %copy.52), channel_id=1, replica_groups=mesh['bx'=32,'by'=2,'col'=2] {'col'}, dimensions={2}, use_global_device_ids=true | all-gather | bytes 496128 | tf_op jit(solution)/shard_map/all_gather | solution.py:75
  148.5 1.4 copy.72
  149.9 1.6 copy.74
  151.5 7.1 %fusion = f32[16,17,2,76]{3,2,1,0:T(2,128)S(1)} fusion(bf16[1,1,16,17,76,152]{4,5,3,2,1,0:T(8,128)(2,1)} %copy.75, bf16[1,2,152,1,16,17]{2,1,5,4,3,0:T(2,128)(2,1)S(1)} %copy.72), kind=kOutput, calls=%fused_computation | convolution fusion | flops 12568576 | bytes 6615040 | tf_op jit(solution)/shard_map/abkij,rjabk->riabk/dot_general | solution.py:70
  158.6 7.1 %fusion.2 = f32[16,17,2,76]{3,2,1,0:T(2,128)S(1)} fusion(bf16[1,1,16,17,76,152]{4,5,3,2,1,0:T(8,128)(2,1)} %copy.75, bf16[1,2,152,1,16,17]{2,1,5,4,3,0:T(2,128)(2,1)S(1)} %copy.74), kind=kOutput, calls=%fused_computation.2 | convolution fusion | flops 12568576 | bytes 6615040 | tf_op jit(solution)/shard_map/abkij,rjabk->riabk/dot_general | solution.py:67
  165.7 3.0 %fusion.24 = f32[2,76,16,17]{1,0,3,2:T(2,128)S(1)} fusion(f32[16,17,2,76]{3,2,1,0:T(2,128)S(1)} %fusion.2, bf16[1,1,16,17,76,152]{4,5,3,2,1,0:T(8,128)(2,1)S(1)} %bitcast.198, bf16[1,2,152,1,16,17]{2,1,5,4,3,0:T(2,128)(2,1)S(1)} %copy.72), kind=kOutput, calls=%fused_computation.33 | convolution fusion | flops 12609920 | bytes 6780416 | tf_op jit(solution)/shard_map/abkij,rjabk->riabk/dot_general | solution.py:65
  170.1 3.0 %fusion.30 = f32[2,76,16,17]{1,0,3,2:T(2,128)S(1)} fusion(f32[16,17,2,76]{3,2,1,0:T(2,128)S(1)} %fusion, bf16[1,1,16,17,76,152]{4,5,3,2,1,0:T(8,128)(2,1)S(1)} %bitcast.198, bf16[1,2,152,1,16,17]{2,1,5,4,3,0:T(2,128)(2,1)S(1)} %copy.74), kind=kOutput, calls=%fused_computation.35 | convolution fusion | flops 12609920 | bytes 6780416 | tf_op jit(solution)/shard_map/abkij,rjabk->riabk/dot_general | solution.py:68
  175.4 21.2 %all_to_all.135 = f32[2,2,76,1,16,32]{2,4,1,3,0,5:T(8,128)S(1)} all-to-all(f32[2,2,76,1,16,32]{2,4,1,3,0,5:T(8,128)S(1)} %copy.61), channel_id=1, replica_groups=mesh['bx'=32,'by'=2,'col'=2] {'bx'}, dimensions={5} | all-to-all | bytes 1245184 | tf_op jit(solution)/shard_map/all_to_all | solution.py:45
  197.2 18.8 %all_to_all.136 = f32[2,2,76,32,16,1]{2,3,4,0,5,1:T(8,128)S(1)} all-to-all(f32[2,2,76,32,16,1]{2,3,4,0,5,1:T(8,128)S(1)} %copy.62), channel_id=1, replica_groups=mesh['bx'=32,'by'=2,'col'=2] {'by'}, dimensions={1} | all-to-all | bytes 1245184 | tf_op jit(solution)/shard_map/all_to_all | solution.py:44
  220.5 16.1 %all_to_all.137 = f32[1,76,32,32,1]{1,3,4,0,2:T(8,128)S(1)} all-to-all(f32[1,76,32,32,1]{1,3,4,0,2:T(8,128)S(1)} %fusion.10), channel_id=1, replica_groups=mesh['bx'=32,'by'=2,'col'=2] {'bx'}, dimensions={2} | all-to-all | bytes 622592 | tf_op jit(solution)/shard_map/all_to_all | solution.py:55
  236.9 12.3 %all_to_all.138 = f32[1,76,1,32,32]{1,4,2,0,3:T(8,128)S(1)} all-to-all(f32[1,76,1,32,32]{1,4,2,0,3:T(8,128)S(1)} %copy.66), channel_id=1, replica_groups=mesh['bx'=32,'by'=2,'col'=2] {'by'}, dimensions={3} | all-to-all | bytes 622592 | tf_op jit(solution)/shard_map/all_to_all | solution.py:54
  249.2 0.9 copy.67
  (39 shorter events, 14.9 us)
Async XLA Ops:
  57.4 56.5 %all-to-all-start.3 = ((f32[2,1,76,1,32,32]{2,5,0,3,1,4:T(8,128)}), f32[2,1,76,1,32,32]{2,5,0,3,1,4:T(8,128)S(1)}, u32[]{:S(2)}, u32[]{:S(2)}) async-start(f32[2,1,76,1,32,32]{2,5,0,3,1,4:T(8,128)} %copy.50), calls=%async_computation.3 | async-start | bytes 2097152 | tf_op jit(solution)/shard_map/all_to_all | solution.py:34
  151.5 14.2 %slice-start = ((s8[10584064]{0:T(1024)(128)(4,1)}), s8[4194304]{0:T(1024)(128)(4,1)S(1)}, s32[]{:S(2)}) async-start(s8[10584064]{0:T(1024)(128)(4,1)} %bitcast.197), calls=%async_computation.8 | async-start | bytes 8388608
  151.5 14.2 %slice-start.1 = ((s8[10584064]{0:T(1024)(128)(4,1)}), s8[4194304]{0:T(1024)(128)(4,1)S(1)}, s32[]{:S(2)}) async-start(s8[10584064]{0:T(1024)(128)(4,1)} %bitcast.197), calls=%async_computation.9 | async-start | bytes 8388608
  158.6 7.1 %slice-start.2 = ((s8[10584064]{0:T(1024)(128)(4,1)}), s8[2195456]{0:T(1024)(128)(4,1)S(1)}, s32[]{:S(2)}) async-start(s8[10584064]{0:T(1024)(128)(4,1)} %bitcast.197), calls=%async_computation.10 | async-start | bytes 4390912
where the time goes:
time: 251 us; the launch traced here: 250 us
  blocking collectives  148 us (59%)
  local copies, waits for them, and re-layouts  64.4 us (26%)
  matrix products  33.9 us (14%)
  starting transfers between devices  3.58 us (1%)
    unnamed x11, local copies, waits for them, and re-layouts  41.8 us
    all_gather x1, blocking collectives, apply_kernel(): panels = lax.all_gather(spectrum, 'col', axis=2, tiled=True)  29.5 us
    all_to_all x1, blocking collectives, to_columns(): lax.all_to_all(waves, 'bx', split_axis=3, concat_axis=5, tiled=True)  21.3 us
    all_to_all x1, blocking collectives, back_planes(): lax.all_to_all(columns, 'bx', split_axis=5, concat_axis=3, tiled=True)  21.2 us
    all_to_all x1, blocking collectives, back_planes(): lax.all_to_all(lax.all_to_all(columns, 'bx', split_axis=5, concat_axis=3,...  18.8 us
    all_to_all x1, blocking collectives, to_planes(): lax.all_to_all(spatial, 'bx', split_axis=4, concat_axis=2, tiled=True)  18.2 us
    all_to_all x1, blocking collectives, back_boxes(): lax.all_to_all(planes, 'bx', split_axis=2, concat_axis=4, tiled=True)  16.1 us
    slice x1, local copies, waits for them, and re-layouts, kernel_terms(): kernel_part[0]  15.2 us
  transfers between devices with their start and end apart: 1, of which 0 were waited for; matrix products, arithmetic and copies ran while one was open for 21% of the time, Pallas kernels for 0%

commit v1 on v0

--- a/solution.py
+++ b/solution.py
@@ -72,7 +72,9 @@
 
 
 def apply_kernel(spectrum, kernel):
-    panels = lax.all_gather(spectrum, "col", axis=2, tiled=True)
+    panels = jnp.concatenate(
+        lax.all_to_all(jnp.stack([spectrum] * lax.axis_size("col")), "col", 0, 0), axis=2
+    )
     return kernel_terms(kernel, panels)
 
 

time: 251 us -> 229 us (0.912)
  blocking collectives: 148 us -> 134 us
  local copies, waits for them, and re-layouts: 64.4 us -> 59.8 us
  matrix products: 33.9 us -> 30 us
    all_gather x1 -> x0, blocking collectives: 29.5 us -> none  [apply_kernel(): panels = lax.all_gather(spectrum, 'col', axis=2, tiled=True)]
    all_to_all x0 -> x1, blocking collectives: none -> 17.5 us  [to_columns(): lax.all_to_all(lax.all_to_all(waves, 'bx', split_axis=3, concat_axis=5, t...]
    dot_general x1, matrix products: 7.08 us -> 2.93 us  [kernel_terms(): jnp.einsum(pattern, kernel_part[1], panel[1], preferred_element_type=jnp....]
    unnamed x11, local copies, waits for them, and re-layouts: 41.8 us -> 39.1 us
  transfers between devices with their start and end apart: 1 -> 1, of which waited for: 0 -> 0; matrix products, arithmetic and copies ran while one was open for 21% -> 23% of each run, Pallas kernels for 0% -> 0%
where the time goes in v1:
time: 229 us; the launch traced here: 228 us
  blocking collectives  134 us (59%)
  local copies, waits for them, and re-layouts  59.8 us (26%)
  matrix products  30 us (13%)
  starting transfers between devices  3.49 us (2%)
    unnamed x11, local copies, waits for them, and re-layouts  39.1 us
    all_to_all x1, blocking collectives, to_columns(): lax.all_to_all(waves, 'bx', split_axis=3, concat_axis=5, tiled=True)  21.3 us
    all_to_all x1, blocking collectives, back_planes(): lax.all_to_all(columns, 'bx', split_axis=5, concat_axis=3, tiled=True)  21.2 us
    all_to_all x1, blocking collectives, to_planes(): lax.all_to_all(spatial, 'bx', split_axis=4, concat_axis=2, tiled=True)  18.2 us
    all_to_all x1, blocking collectives, to_columns(): lax.all_to_all(lax.all_to_all(waves, 'bx', split_axis=3, concat_axis=5, t...  17.5 us
    all_to_all x1, blocking collectives, back_planes(): lax.all_to_all(lax.all_to_all(columns, 'bx', split_axis=5, concat_axis=3,...  17.5 us
    all_to_all x1, blocking collectives, back_boxes(): lax.all_to_all(planes, 'bx', split_axis=2, concat_axis=4, tiled=True)  15.9 us
    slice x1, local copies, waits for them, and re-layouts, kernel_terms(): kernel_part[0]  15.2 us
  transfers between devices with their start and end apart: 1, of which 0 were waited for; matrix products, arithmetic and copies ran while one was open for 23% of the time, Pallas kernels for 0%

profile of v1, /device:TPU:1, one launch (start us, length us, event | category | flops | bytes accessed | tf_op | source)
XLA Modules:
  0.0 228.1 jit_solution(10128571044007991757)
XLA Ops:
  0.0 1.1 copy.40
  1.2 18.2 %all_to_all.137 = bf16[2,76,1,16,32]{1,3,0,2,4:T(8,128)(2,1)S(1)} all-to-all(bf16[2,76,1,16,32]{1,3,0,2,4:T(8,128)(2,1)S(1)} %copy.41), channel_id=1, replica_groups=mesh['bx'=32,'by'=2,'col'=2] {'bx'}, dimensions={4} | all-to-all | bytes 311296 | tf_op jit(solution)/shard_map/all_to_all | solution.py:25
  19.5 10.3 %all_to_all.138 = bf16[2,76,32,16,1]{1,2,3,4,0:T(8,128)(2,1)S(1)} all-to-all(bf16[2,76,32,16,1]{1,2,3,4,0:T(8,128)(2,1)S(1)} %copy.42), channel_id=1, replica_groups=mesh['bx'=32,'by'=2,'col'=2] {'by'}, dimensions={0} | all-to-all | bytes 311296 | tf_op jit(solution)/shard_map/all_to_all | solution.py:24
  31.6 0.9 fusion.38
  32.5 0.9 fusion.16
  33.4 0.9 fusion.15
  34.5 21.3 %all_to_all.139 = f32[2,1,76,32,32,1]{2,4,5,1,0,3:T(8,128)S(1)} all-to-all(f32[2,1,76,32,32,1]{2,4,5,1,0,3:T(8,128)S(1)} %copy.47), channel_id=1, replica_groups=mesh['bx'=32,'by'=2,'col'=2] {'bx'}, dimensions={3} | all-to-all | bytes 1245184 | tf_op jit(solution)/shard_map/all_to_all | solution.py:35
  56.4 17.5 %all_to_all.140 = f32[2,1,76,1,32,32]{2,5,0,3,1,4:T(8,128)S(1)} all-to-all(f32[2,1,76,1,32,32]{2,5,0,3,1,4:T(8,128)S(1)} %copy.48), channel_id=1, replica_groups=mesh['bx'=32,'by'=2,'col'=2] {'by'}, dimensions={4} | all-to-all | bytes 1245184 | tf_op jit(solution)/shard_map/all_to_all | solution.py:34
  76.5 0.9 copy.50
  77.4 3.5 %all-to-all-start.4 = ((bf16[2,2,2,76,1,16,17]{3,5,6,4,2,1,0:T(8,128)(2,1)}), bf16[2,2,2,76,1,16,17]{3,5,6,4,2,1,0:T(8,128)(2,1)S(1)}, u32[]{:S(2)}, u32[]{:S(2)}) async-start(bf16[2,2,2,76,1,16,17]{3,5,6,4,2,1,0:T(8,128)(2,1)} %copy.50), calls=%async_computation.4 | async-start | bytes 1114112 | tf_op jit(solution)/shard_map/all_to_all | solution.py:76
  80.9 15.2 %fusion.196 = (bf16[1,1,16,17,76,152]{5,2,4,3,1,0:T(8,128)(2,1)}, bf16[1,1,16,17,76,152]{5,2,4,3,1,0:T(8,128)(2,1)}) fusion(bf16[2,1,16,17,76,152]{5,2,4,3,1,0:T(8,128)(2,1)} %param.3), kind=kLoop, calls=%fused_computation.191 | loop fusion | bytes 25137152 | tf_op jit(solution)/shard_map/slice | solution.py:66
  96.0 18.8 %copy.78 = bf16[1,1,16,17,76,152]{4,5,3,2,1,0:T(8,128)(2,1)} copy(bf16[1,1,16,17,76,152]{5,2,4,3,1,0:T(8,128)(2,1)} %get-tuple-element.5) | data formatting | bytes 12568576
  114.9 18.8 %copy.79 = bf16[1,1,16,17,76,152]{4,5,3,2,1,0:T(8,128)(2,1)} copy(bf16[1,1,16,17,76,152]{5,2,4,3,1,0:T(8,128)(2,1)} %get-tuple-element.6) | data formatting | bytes 12568576
  135.0 7.1 %fusion = f32[16,17,2,76]{3,2,1,0:T(2,128)S(1)} fusion(bf16[2,152,16,17]{1,0,3,2:T(2,128)(2,1)S(1)} %reshape.215, bf16[1,1,16,17,76,152]{4,5,3,2,1,0:T(8,128)(2,1)} %copy.79), kind=kOutput, calls=%fused_computation | convolution fusion | flops 12568576 | bytes 6615040 | tf_op jit(solution)/shard_map/abkij,rjabk->riabk/dot_general | solution.py:70
  142.0 2.9 %fusion.2 = f32[16,17,2,76]{3,2,1,0:T(2,128)S(1)} fusion(bf16[2,152,16,17]{1,0,3,2:T(2,128)(2,1)S(1)} %reshape.216, bf16[1,1,16,17,76,152]{4,5,3,2,1,0:T(8,128)(2,1)S(1)} %copy-done), kind=kOutput, calls=%fused_computation.2 | convolution fusion | flops 12568576 | bytes 6615040 | tf_op jit(solution)/shard_map/abkij,rjabk->riabk/dot_general | solution.py:67
  145.2 3.0 %fusion.24 = f32[2,76,16,17]{1,0,3,2:T(2,128)S(1)} fusion(f32[16,17,2,76]{3,2,1,0:T(2,128)S(1)} %fusion.2, bf16[2,152,16,17]{1,0,3,2:T(2,128)(2,1)S(1)} %reshape.215, bf16[1,1,16,17,76,152]{4,5,3,2,1,0:T(8,128)(2,1)S(1)} %bitcast.197), kind=kOutput, calls=%fused_computation.33 | convolution fusion | flops 12609920 | bytes 6780416 | tf_op jit(solution)/shard_map/abkij,rjabk->riabk/dot_general | solution.py:65
  149.6 3.0 %fusion.30 = f32[2,76,16,17]{1,0,3,2:T(2,128)S(1)} fusion(f32[16,17,2,76]{3,2,1,0:T(2,128)S(1)} %fusion, bf16[2,152,16,17]{1,0,3,2:T(2,128)(2,1)S(1)} %reshape.216, bf16[1,1,16,17,76,152]{4,5,3,2,1,0:T(8,128)(2,1)S(1)} %bitcast.197), kind=kOutput, calls=%fused_computation.35 | convolution fusion | flops 12609920 | bytes 6780416 | tf_op jit(solution)/shard_map/abkij,rjabk->riabk/dot_general | solution.py:68
  153.3 0.9 fusion.14
  154.9 21.2 %all_to_all.141 = f32[2,2,76,1,16,32]{2,4,1,3,0,5:T(8,128)S(1)} all-to-all(f32[2,2,76,1,16,32]{2,4,1,3,0,5:T(8,128)S(1)} %copy.63), channel_id=1, replica_groups=mesh['bx'=32,'by'=2,'col'=2] {'bx'}, dimensions={5} | all-to-all | bytes 1245184 | tf_op jit(solution)/shard_map/all_to_all | solution.py:45
  176.7 17.5 %all_to_all.142 = f32[2,2,76,32,16,1]{2,3,4,0,5,1:T(8,128)S(1)} all-to-all(f32[2,2,76,32,16,1]{2,3,4,0,5,1:T(8,128)S(1)} %copy.64), channel_id=1, replica_groups=mesh['bx'=32,'by'=2,'col'=2] {'by'}, dimensions={1} | all-to-all | bytes 1245184 | tf_op jit(solution)/shard_map/all_to_all | solution.py:44
  197.9 0.9 fusion.10
  198.8 15.9 %all_to_all.143 = f32[1,76,32,32,1]{1,3,4,0,2:T(8,128)S(1)} all-to-all(f32[1,76,32,32,1]{1,3,4,0,2:T(8,128)S(1)} %fusion.10), channel_id=1, replica_groups=mesh['bx'=32,'by'=2,'col'=2] {'bx'}, dimensions={2} | all-to-all | bytes 622592 | tf_op jit(solution)/shard_map/all_to_all | solution.py:55
  214.9 12.3 %all_to_all.144 = f32[1,76,1,32,32]{1,4,2,0,3:T(8,128)S(1)} all-to-all(f32[1,76,1,32,32]{1,4,2,0,3:T(8,128)S(1)} %copy.68), channel_id=1, replica_groups=mesh['bx'=32,'by'=2,'col'=2] {'by'}, dimensions={3} | all-to-all | bytes 622592 | tf_op jit(solution)/shard_map/all_to_all | solution.py:54
  227.2 0.9 copy.69
  (43 shorter events, 13.9 us)
Async XLA Ops:
  77.4 56.4 %all-to-all-start.4 = ((bf16[2,2,2,76,1,16,17]{3,5,6,4,2,1,0:T(8,128)(2,1)}), bf16[2,2,2,76,1,16,17]{3,5,6,4,2,1,0:T(8,128)(2,1)S(1)}, u32[]{:S(2)}, u32[]{:S(2)}) async-start(bf16[2,2,2,76,1,16,17]{3,5,6,4,2,1,0:T(8,128)(2,1)} %copy.50), calls=%async_computation.4 | async-start | bytes 1114112 | tf_op jit(solution)/shard_map/all_to_all | solution.py:76
  134.9 7.1 %copy-start = (bf16[1,1,16,17,76,152]{4,5,3,2,1,0:T(8,128)(2,1)S(1)}, bf16[1,1,16,17,76,152]{4,5,3,2,1,0:T(8,128)(2,1)}, u32[]{:S(2)}) copy-start(bf16[1,1,16,17,76,152]{4,5,3,2,1,0:T(8,128)(2,1)} %copy.79) | copy-start | bytes 18852868
  134.9 10.0 %slice-start = ((s8[10584064]{0:T(1024)(128)(4,1)}), s8[4194304]{0:T(1024)(128)(4,1)S(1)}, s32[]{:S(2)}) async-start(s8[10584064]{0:T(1024)(128)(4,1)} %bitcast.196), calls=%async_computation.9 | async-start | bytes 8388608
  135.0 10.0 %slice-start.1 = ((s8[10584064]{0:T(1024)(128)(4,1)}), s8[4194304]{0:T(1024)(128)(4,1)S(1)}, s32[]{:S(2)}) async-start(s8[10584064]{0:T(1024)(128)(4,1)} %bitcast.196), calls=%async_computation.10 | async-start | bytes 8388608
  142.0 3.2 %slice-start.2 = ((s8[10584064]{0:T(1024)(128)(4,1)}), s8[2195456]{0:T(1024)(128)(4,1)S(1)}, s32[]{:S(2)}) async-start(s8[10584064]{0:T(1024)(128)(4,1)} %bitcast.196), calls=%async_computation.11 | async-start | bytes 4390912
